TPU v7x, 128 devices: a whole 4x4x4 slice. The times are simulated.
128 devices in a mesh: segment: 4 (over x), tensor: 32 (over z, y, core).
Axes of the slice: x: 4, y: 4, z: 4, core: 2. Of those that a mesh axis runs over, the one named last changes fastest.
Arguments:
- hidden: bfloat16 [4, 2, 768, 3072], P('segment', None, 'tensor'), may hold values from -6 to 6
- gate_weight: bfloat16 [4, 3072, 16384], P('segment', None, 'tensor'), may hold values from -0.109375 to 0.109375
- up_weight: bfloat16 [4, 3072, 16384], P('segment', None, 'tensor'), may hold values from -0.109375 to 0.109375
- down_weight: bfloat16 [4, 16384, 3072], P('segment', 'tensor'), may hold values from -0.046875 to 0.046875
- block_rows: int32 [4, 2, 6, 128], P('segment'), may hold values from 0 to 768, as said below
- slot_gate: float32 [4, 2, 6, 128], P('segment'), may hold values from 0.1 to 1
Outputs:
- handed: bfloat16 [4, 2, 768, 3072], P('segment', None, 'tensor')
Inputs may be any that keep to these rules, and one draw needn't show every extreme that they name: `block_rows`: each entry is a token row of its micro-batch or 768 for an empty slot. Within one list of 768 slots the named rows are distinct and ascending and the empty slots come last; a list holds from 307 to 768 live slots, and both ends occur in every draw.
All inputs are finite; a program needn't handle non-finite values.
Results may differ from a plain program's by a relative error of at most 0.0085.
Values may be sent and summed in bfloat16 or wider, within the bound.
A program may use at most 128 MiB of HBM per device.

v0:
```python
import jax
import jax.numpy as jnp
from jax import lax
from jax.sharding import PartitionSpec as P


def from_behind(value, axis, steps):
    count = lax.axis_size(axis)
    pairs = [(source, (source + steps) % count) for source in range(count)]
    return lax.ppermute(value, axis, pairs)


def per_device(hidden, gate_weight, up_weight, down_weight, block_rows, slot_gate):
    batches, shard_rows, features = hidden.shape[1:]
    count = lax.axis_size("tensor")
    own = hidden[0].reshape(batches * shard_rows, features)
    gathered = lax.all_gather(own, "tensor", axis=0, tiled=True)
    token = jnp.arange(count * shard_rows)
    hit = block_rows[0].reshape(batches, 1, -1) == token[None, :, None]
    gates = jnp.sum(jnp.where(hit, slot_gate[0].reshape(batches, 1, -1), 0.0), axis=2)
    column = gates.reshape(batches, count, shard_rows).transpose(1, 0, 2).reshape(-1, 1)
    gate_act = jnp.dot(gathered, gate_weight[0], preferred_element_type=jnp.float32)
    up_act = jnp.dot(gathered, up_weight[0], preferred_element_type=jnp.float32)
    hidden_act = (jax.nn.silu(gate_act) * up_act).astype(jnp.bfloat16)
    part = jnp.dot(hidden_act, down_weight[0], preferred_element_type=jnp.float32) * column
    summed = lax.psum_scatter(part.astype(jnp.bfloat16), "tensor", scatter_dimension=0, tiled=True)
    updated = (own.astype(jnp.float32) + summed.astype(jnp.float32)).astype(jnp.bfloat16)
    return from_behind(updated.reshape(hidden.shape), "segment", 1)


def solution(mesh):
    return jax.shard_map(
        per_device,
        mesh=mesh,
        in_specs=(
            P("segment", None, "tensor", None),
            P("segment", None, "tensor"),
            P("segment", None, "tensor"),
            P("segment", "tensor", None),
            P("segment", None, None, None),
            P("segment", None, None, None),
        ),
        out_specs=P("segment", None, "tensor", None),
        check_vma=False,
    )
```

profile of v0, /device:TPU:0, one launch (start us, length us, event | category | flops | bytes accessed | tf_op | source)
XLA Modules:
  0.0 206.5 jit_solution(4365729966187705656)
XLA Ops:
  6.5 0.0 copy-start
  6.5 0.0 all-gather.2.cloned.1.call-start
  6.5 0.7 all-gather.2.cloned.1.call-update
  7.3 0.0 reduce-scatter.2.cloned.1.call-start
  7.3 1.5 select_reduce_fusion
  8.8 0.1 reshape.10
  8.9 0.1 mul.19
  9.0 58.4 %all-gather.2.cloned.1.call-done = bf16[1536,3072]{1,0:T(8,128)(2,1)} async-done(((bf16[48,3072]{1,0:T(8,128)(2,1)}), bf16[1536,3072]{1,0:T(8,128)(2,1)}) %all-gather.2.cloned.1.call-update) | async-done | bytes 9437200 | tf_op jit(solution)/shard_map/all_gather | solution.py:17
  67.4 10.6 %fusion.2 = f32[1536,512]{1,0:T(8,128)} fusion(bf16[1536,3072]{1,0:T(8,128)(2,1)} %all-gather.2.cloned.1.call-done, bf16[1,3072,512]{2,1,0:T(8,128)(2,1)} %param.7), kind=kOutput, calls=%fused_computation.6 | convolution fusion | flops 4831838208 | bytes 15728640 | tf_op jit(solution)/shard_map/dot_general | solution.py:22
  78.0 0.0 copy-done
  78.0 16.3 %multiply_convert_fusion = bf16[1536,3072]{1,0:T(8,128)(2,1)} fusion(f32[1536]{0:T(1024)S(1)} %mul.19, bf16[1,512,3072]{2,1,0:T(8,128)(2,1)S(1)} %copy-done, bf16[1536,3072]{1,0:T(8,128)(2,1)} %all-gather.2.cloned.1.call-done, bf16[1,3072,512]{2,1,0:T(8,128)(2,1)} %param.8, f32[1536,512]{1,0:T(8,128)} %fusion.2), kind=kOutput, calls=%fused_computation | convolution fusion | flops 9677832192 | bytes 28317696 | tf_op jit(solution)/shard_map/dot_general | solution.py:25
  94.4 0.0 copy-start.1
  94.4 0.0 reduce-scatter.2.cloned.1.call-update
  94.4 95.3 %reduce-scatter.2.cloned.1.call-done = bf16[48,3072]{1,0:T(8,128)(2,1)} async-done(((bf16[1536,3072]{1,0:T(8,128)(2,1)}), bf16[48,3072]{1,0:T(8,128)(2,1)}) %reduce-scatter.2.cloned.1.call-update) | async-done | bytes 294928 | tf_op jit(solution)/shard_map/reduce_scatter | solution.py:26
  189.7 0.0 copy-done.1
  189.7 1.0 add_convert_fusion
  190.7 1.5 collective-permute-start
  192.3 6.7 %collective-permute-done = bf16[1,2,24,3072]{3,2,1,0:T(8,128)(2,1)S(1)} collective-permute-done((bf16[1,2,24,3072]{3,2,1,0:T(8,128)(2,1)S(1)}, bf16[1,2,24,3072]{3,2,1,0:T(8,128)(2,1)S(1)}, u32[]{:S(2)}, u32[]{:S(2)}) %collective-permute-start) | collective-permute-done | bytes 294944 | tf_op jit(solution)/shard_map/ppermute | solution.py:10
  198.9 0.7 copy.10
  (1 shorter events, 0.0 us)
Async XLA Ops:
  6.5 71.5 %copy-start = (bf16[1,512,3072]{2,1,0:T(8,128)(2,1)S(1)}, bf16[1,512,3072]{2,1,0:T(8,128)(2,1)}, u32[]{:S(2)}) copy-start(bf16[1,512,3072]{2,1,0:T(8,128)(2,1)} %param.9) | copy-start | bytes 9437188
  6.5 60.9 %all-gather.2.cloned.1.call-start = ((), (), s32[]{:S(2)}) async-start(), calls=%async_computation.1 | async-start | bytes 9732096 | tf_op jit(solution)/shard_map/all_gather | solution.py:17
  7.3 182.4 %reduce-scatter.2.cloned.1.call-start = ((), (), s32[]{:S(2)}) async-start(), calls=%async_computation.2 | async-start | bytes 9732096 | tf_op jit(solution)/shard_map/reduce_scatter | solution.py:26
  94.4 95.3 %copy-start.1 = (bf16[1,2,24,3072]{3,2,1,0:T(8,128)(2,1)S(1)}, bf16[1,2,24,3072]{3,2,1,0:T(8,128)(2,1)}, u32[]{:S(2)}) copy-start(bf16[1,2,24,3072]{3,2,1,0:T(8,128)(2,1)} %param.6) | copy-start | bytes 884740
  190.7 8.2 %collective-permute-start = (bf16[1,2,24,3072]{3,2,1,0:T(8,128)(2,1)S(1)}, bf16[1,2,24,3072]{3,2,1,0:T(8,128)(2,1)S(1)}, u32[]{:S(2)}, u32[]{:S(2)}) collective-permute-start(bf16[1,2,24,3072]{3,2,1,0:T(8,128)(2,1)S(1)} %bitcast.22), channel_id=1, source_target_pairs={{0,32},{32,64},{64,96},{96,0},{1,33},{33,65},{65,97},{97,1},{2,34}... | collective-permute-start | bytes 884744 | tf_op jit(solution)/shard_map/ppermute | solution.py:10
Sparse Core Ops, SparseCore 0:
  9.6 57.8 all-gather.1
  94.5 95.1 reduce-scatter.1
where the time goes:
time: 207 us; the launch traced here: 206 us
  waiting for transfers between devices  161 us (78%)
  matrix products  26.9 us (13%)
  between operations  13.4 us (6%)
  other arithmetic  2.53 us (1%)
    reduce_scatter x1, waiting for transfers between devices, per_device(): lax.psum_scatter(part.astype(jnp.bfloat16), 'tensor', scatter_dimension=0...  95.3 us
    all_gather x1, waiting for transfers between devices, per_device(): gathered = lax.all_gather(own, 'tensor', axis=0, tiled=True)  58.4 us
    dot_general x1, matrix products, per_device(): jnp.dot(hidden_act, down_weight[0], preferred_element_type=jnp.float32)  16.3 us
    dot_general x1, matrix products, per_device(): jnp.dot(gathered, gate_weight[0], preferred_element_type=jnp.float32)  10.6 us
    ppermute x1, waiting for transfers between devices, from_behind(): return lax.ppermute(value, axis, pairs)  6.69 us
  transfers between devices with their start and end apart: 3, of which 3 were waited for; matrix products, arithmetic and copies ran while one was open for 1% of the time, Pallas kernels for 0%

commit v1 on v0

v1 whole, which is shorter than its diff:
```python
import jax
import jax.numpy as jnp
from jax import lax
from jax.experimental import pallas as pl
from jax.experimental.pallas import tpu as pltpu
from jax.sharding import PartitionSpec as P

MESH = pl.DeviceIdType.MESH
SIDE = 4
COPIES = 96


def kernel(
    segments, batches,
    h_ref, wg_ref, wu_ref, wd_ref, rows_ref, gates_ref, out_ref,
    x, o, rp, ra, rb, ru, rv, fa, fb, fu, fv, fin, wg, wu, wd, act, gcol,
    local_sem, send_sem, recv_sem,
):
    f32, bf16 = jnp.float32, jnp.bfloat16
    rows, width = h_ref.shape
    shard = rows // batches
    half = width // 2
    group = SIDE * rows
    units = wg.shape[1]
    seg, me = lax.axis_index("segment"), lax.axis_index("tensor")
    core = lax.rem(me, 2)
    y = lax.rem(lax.div(me, 2), SIDE)
    z = lax.div(me, 2 * SIDE)

    def member(c, d, e):
        dy = d * (1 - c) + e * c
        dz = e * (1 - c) + d * c
        return (lax.rem(z + dz, SIDE) * SIDE + lax.rem(y + dy, SIDE)) * 2 + c

    first_up, first_down = (seg, member(core, 1, 0)), (seg, member(core, SIDE - 1, 0))
    second_up, second_down = (seg, member(core, 0, 1)), (seg, member(core, 0, SIDE - 1))
    partner = (seg, me + 1 - 2 * core)
    ahead = (lax.rem(seg + 1, segments), me)
    behind = (lax.rem(seg + segments - 1, segments), me)

    cols = (pl.ds(0, half), pl.ds(half, half))
    everything = pl.ds(0, width)

    def slot(ref, f, d, e, part=everything):
        return ref.at[pl.ds(((f * SIDE + d) * SIDE + e) * rows, rows), part]

    def line(ref, d, *part):
        return ref.at[(pl.ds(d * rows, rows), *part)]

    used = []

    def copy(src, dst, device):
        k = len(used)
        made = pltpu.make_async_remote_copy(
            src_ref=src, dst_ref=dst, send_sem=send_sem.at[k], recv_sem=recv_sem.at[k],
            device_id=device, device_id_type=MESH,
        )
        used.append(made)
        return made

    def start(*made):
        for one in made:
            one.start()

    def arrived(*made):
        for one in made:
            one.wait_recv()

    p1p = copy(slot(x, 0, 0, 0), slot(x, 0, 3, 0), first_up)
    p1m = copy(slot(x, 0, 0, 0), slot(x, 0, 1, 0), first_down)
    p2p = copy(slot(x, 0, 3, 0, cols[0]), slot(x, 0, 2, 0, cols[0]), first_up)
    p2m = copy(slot(x, 0, 1, 0, cols[1]), slot(x, 0, 2, 0, cols[1]), first_down)
    qap = [copy(slot(x, 0, d, 0), slot(x, 0, d, 3), second_up) for d in range(SIDE)]
    qam = [copy(slot(x, 0, d, 0), slot(x, 0, d, 1), second_down) for d in range(SIDE)]
    qbp = [copy(slot(x, 0, d, 3, cols[0]), slot(x, 0, d, 2, cols[0]), second_up) for d in range(SIDE)]
    qbm = [copy(slot(x, 0, d, 1, cols[1]), slot(x, 0, d, 2, cols[1]), second_down) for d in range(SIDE)]
    over = [[copy(slot(x, 0, d, e), slot(x, 1, d, e), partner) for e in range(SIDE)] for d in range(SIDE)]

    def band(ref, f, d, part):
        return ref.at[pl.ds((f * SIDE + d) * group, group), part]

    back = [[copy(band(o, 1, d, c), band(rp, 0, d, c), partner) for c in cols] for d in range(SIDE)]
    r1p = [copy(slot(o, 0, d, 2, cols[0]), line(ra, d), second_up) for d in range(SIDE)]
    r1m = [copy(slot(o, 0, d, 2, cols[1]), line(rb, d), second_down) for d in range(SIDE)]
    r2p = [[copy(slot(o, 0, d, 1, c), line(ru, d, c), second_up) for c in cols] for d in range(SIDE)]
    r2m = [[copy(slot(o, 0, d, 3, c), line(rv, d, c), second_down) for c in cols] for d in range(SIDE)]
    f1p = copy(slot(o, 0, 2, 0, cols[0]), fa, first_up)
    f1m = copy(slot(o, 0, 2, 0, cols[1]), fb, first_down)
    f2p = [copy(slot(o, 0, 1, 0, c), fu.at[:, c], first_up) for c in cols]
    f2m = [copy(slot(o, 0, 3, 0, c), fv.at[:, c], first_down) for c in cols]
    hand = [copy(fin.at[:, c], out_ref.at[:, c], ahead) for c in cols]

    own = pltpu.make_async_copy(h_ref, slot(x, 0, 0, 0), local_sem.at[0])
    own.start()
    loads = [
        pltpu.make_async_copy(src, dst, local_sem.at[1 + k])
        for k, (src, dst) in enumerate(((wg_ref, wg), (wu_ref, wu), (wd_ref, wd)))
    ]
    start(*loads)

    barrier = pltpu.get_barrier_semaphore()
    near = (first_up, first_down, second_up, second_down, partner, ahead, behind)
    for device in near:
        pl.semaphore_signal(barrier, inc=1, device_id=device, device_id_type=MESH)
    pl.semaphore_wait(barrier, len(near))
    own.wait()
    start(p1p, p1m, over[0][0])

    def gate_of(k, carry):
        f = lax.div(k, SIDE * SIDE)
        source = member(core + f - 2 * core * f, lax.rem(lax.div(k, SIDE), SIDE), lax.rem(k, SIDE))
        token = lax.broadcasted_iota(jnp.int32, (shard, 128), 0) + source * shard
        for b in range(batches):
            total = jnp.zeros((shard, 128), f32)
            for block in range(rows_ref.shape[0]):
                named = rows_ref[block, b : b + 1, :]
                total += jnp.where(token == named, gates_ref[block, b : b + 1, :], 0.0)
            at = pl.multiple_of(k * rows + b * shard, 8)
            gcol[pl.ds(at, shard), :] = jnp.broadcast_to(
                jnp.sum(total, axis=1, keepdims=True), (shard, 128)
            )
        return carry

    lax.fori_loop(0, 2 * SIDE * SIDE, gate_of, 0)

    arrived(p1p)
    start(p2p)
    arrived(p1m)
    start(p2m, qap[0], qam[0], over[3][0], over[1][0])
    arrived(p2p, p2m)
    start(qap[2], qam[2], over[2][0])
    arrived(qap[0])
    start(qbp[0], over[0][3])
    arrived(qam[0])
    start(qbm[0], over[0][1], qap[1], qam[1])
    arrived(qap[2])
    start(qbp[2], over[2][3])
    arrived(qam[2])
    start(qbm[2], over[2][1], qap[3], qam[3])
    arrived(qbp[0], qbm[0])
    start(over[0][2])
    for load in loads:
        load.wait()

    step = min(256, units)
    wide = min(512, half)

    def first(f, d, n):
        at = (f * SIDE + d) * group
        tokens = x[pl.ds(at, group), :]
        part = pl.ds(n * step, step)
        g = jnp.dot(tokens, wg[:, part], preferred_element_type=f32)
        u = jnp.dot(tokens, wu[:, part], preferred_element_type=f32)
        gate = gcol[pl.ds(at, group), :]
        gate = jnp.concatenate([gate] * (step // 128), axis=1)
        act[f, :, part] = (g / (1.0 + jnp.exp(-g)) * u * gate).astype(bf16)

    def second(f, d, h):
        at = (f * SIDE + d) * group
        for n in range(half // wide):
            part = pl.ds(h * half + n * wide, wide)
            term = jnp.dot(act[f], wd[:, part], preferred_element_type=f32)
            if f == 0:
                term = term + rp[pl.ds(d * group, group), part].astype(f32)
            o[pl.ds(at, group), part] = term.astype(bf16)

    def add(into, *terms):
        total = into[...].astype(f32)
        for term in terms:
            total = total + term[...].astype(f32)
        into[...] = total.astype(bf16)

    def relay(d):
        arrived(r1p[d])
        add(slot(o, 0, d, 1, cols[0]), line(ra, d))
        start(r2p[d][0])
        arrived(r1m[d])
        add(slot(o, 0, d, 3, cols[1]), line(rb, d))
        start(r2m[d][1])

    def settle(d, h):
        arrived(r2p[d][h], r2m[d][h])
        add(slot(o, 0, d, 0, cols[h]), line(ru, d, cols[h]), line(rv, d, cols[h]))

    def nothing():
        pass

    def block(d, hooks, send):
        run = lambda k: hooks.get(k, nothing)()
        arrived(*over[d])
        first(1, d, 0)
        run(0)
        for n in range(1, units // step):
            first(1, d, n)
        run(1)
        second(1, d, 0)
        start(back[d][0])
        run(2)
        second(1, d, 1)
        start(back[d][1])
        run(3)
        first(0, d, 0)
        run(4)
        for n in range(1, units // step):
            first(0, d, n)
        run(5)
        arrived(back[d][0])
        second(0, d, 0)
        if send:
            start(r1p[d], r2m[d][0])
        run(6)
        arrived(back[d][1])
        second(0, d, 1)
        if send:
            start(r1m[d], r2p[d][1])
        run(7)

    def pass_on(d):
        arrived(qap[d])
        start(qbp[d], over[d][3])
        arrived(qam[d])
        start(qbm[d], over[d][1])

    def complete(d):
        arrived(qbp[d], qbm[d])
        start(over[d][2])

    def two_away():
        settle(2, 0)
        settle(2, 1)
        start(f1p, f1m)

    block(0, {5: lambda: pass_on(1), 7: lambda: complete(2)}, False)
    block(2, {4: lambda: pass_on(3), 7: lambda: complete(1)}, True)
    block(1, {0: lambda: complete(3), 4: lambda: relay(2)}, True)
    block(3, {1: two_away, 4: lambda: relay(1)}, True)
    start(r1p[0], r2m[0][0], r1m[0], r2p[0][1])
    settle(1, 0)
    settle(1, 1)
    start(f2p[1])
    arrived(f1p)
    add(slot(o, 0, 1, 0, cols[0]), fa)
    start(f2p[0])
    relay(3)
    relay(0)
    settle(3, 0)
    start(f2m[0])
    settle(3, 1)
    arrived(f1m)
    add(slot(o, 0, 3, 0, cols[1]), fb)
    start(f2m[1])
    for h in (1, 0):
        c = cols[h]
        settle(0, h)
        arrived(f2p[h], f2m[h])
        fin[:, c] = (
            slot(o, 0, 0, 0, c)[...].astype(f32)
            + fu[:, c].astype(f32)
            + fv[:, c].astype(f32)
            + slot(x, 0, 0, 0, c)[...].astype(f32)
        ).astype(bf16)
        start(hand[h])
    arrived(*hand)
    for made in used:
        made.wait_send()


def per_device(hidden, gate_weight, up_weight, down_weight, block_rows, slot_gate):
    batches, shard, width = hidden.shape[1:]
    rows = batches * shard
    units = gate_weight.shape[2]
    segments = lax.axis_size("segment")
    bf16 = jnp.bfloat16
    anywhere, vmem = pl.BlockSpec(memory_space=pl.ANY), pl.BlockSpec(memory_space=pltpu.VMEM)

    def body(*refs):
        kernel(segments, batches, *refs)

    handed = pl.pallas_call(
        body,
        out_shape=jax.ShapeDtypeStruct((rows, width), bf16),
        in_specs=[anywhere] * 4 + [vmem] * 2,
        out_specs=anywhere,
        scratch_shapes=[
            pltpu.VMEM((32 * rows, width), bf16),
            pltpu.VMEM((32 * rows, width), bf16),
            pltpu.VMEM((16 * rows, width), bf16),
            pltpu.VMEM((4 * rows, width // 2), bf16),
            pltpu.VMEM((4 * rows, width // 2), bf16),
            pltpu.VMEM((4 * rows, width), bf16),
            pltpu.VMEM((4 * rows, width), bf16),
            pltpu.VMEM((rows, width // 2), bf16),
            pltpu.VMEM((rows, width // 2), bf16),
            pltpu.VMEM((rows, width), bf16),
            pltpu.VMEM((rows, width), bf16),
            pltpu.VMEM((rows, width), bf16),
            pltpu.VMEM((width, units), bf16),
            pltpu.VMEM((width, units), bf16),
            pltpu.VMEM((units, width), bf16),
            pltpu.VMEM((2, 4 * rows, units), bf16),
            pltpu.VMEM((32 * rows, 128), jnp.float32),
            pltpu.SemaphoreType.DMA((4,)),
            pltpu.SemaphoreType.DMA((COPIES,)),
            pltpu.SemaphoreType.DMA((COPIES,)),
        ],
        compiler_params=pltpu.CompilerParams(
            collective_id=0, has_side_effects=True, vmem_limit_bytes=60 * 1024 * 1024
        ),
    )(
        hidden.reshape(rows, width),
        gate_weight[0],
        up_weight[0],
        down_weight[0],
        block_rows[0].transpose(1, 0, 2),
        slot_gate[0].transpose(1, 0, 2),
    )
    return handed.reshape(hidden.shape)


def solution(mesh):
    return jax.shard_map(
        per_device,
        mesh=mesh,
        in_specs=(
            P("segment", None, "tensor", None),
            P("segment", None, "tensor"),
            P("segment", None, "tensor"),
            P("segment", "tensor", None),
            P("segment", None, None, None),
            P("segment", None, None, None),
        ),
        out_specs=P("segment", None, "tensor", None),
        check_vma=False,
    )
```

time: 207 us -> 85.1 us (0.41)
  waiting for transfers between devices: 161 us -> 0 us
  Pallas kernels: 0 us -> 83.2 us
  matrix products: 26.9 us -> 0 us
  between operations: 13.4 us -> 0.01 us
  other arithmetic: 2.53 us -> 0 us
    reduce_scatter x1 -> x0, waiting for transfers between devices: 95.3 us -> none  [per_device(): lax.psum_scatter(part.astype(jnp.bfloat16), 'tensor', scatter_dimension=0...]
    pallas_call x0 -> x1, Pallas kernels: none -> 83.2 us  [per_device(): pl.pallas_call(body, out_shape=jax.ShapeDtypeStruct((rows, width), bf16),...]
    all_gather x1 -> x0, waiting for transfers between devices: 58.4 us -> none  [per_device(): gathered = lax.all_gather(own, 'tensor', axis=0, tiled=True)]
    dot_general x2 -> x0, matrix products: 26.9 us -> none  [the longest x1 16.3 us: per_device(): jnp.dot(hidden_act, down_weight[0], preferred_element_type=jnp.float32)]
    ppermute x1 -> x0, waiting for transfers between devices: 6.69 us -> none  [from_behind(): return lax.ppermute(value, axis, pairs)]
  transfers between devices with their start and end apart: 3 -> 0, of which waited for: 3 -> 0; matrix products, arithmetic and copies ran while one was open for 1% -> 0% of each run, Pallas kernels for 0% -> 0%
where the time goes in v1:
time: 85.1 us; the launch traced here: 85 us
  Pallas kernels  83.2 us (98%)
  local copies, waits for them, and re-layouts  1.69 us (2%)
    pallas_call x1, Pallas kernels, per_device(): pl.pallas_call(body, out_shape=jax.ShapeDtypeStruct((rows, width), bf16),...  83.2 us

profile of v1, /device:TPU:0, one launch (start us, length us, event | category | flops | bytes accessed | tf_op | source)
XLA Modules:
  0.0 85.0 jit_solution(14017265057617858753)
XLA Ops:
  0.0 83.2 %shard_map.64 = bf16[48,3072]{1,0:T(8,128)(2,1)} custom-call(bf16[48,3072]{1,0:T(8,128)(2,1)} %bitcast.15, bf16[3072,512]{1,0:T(8,128)(2,1)} %bitcast.11, bf16[3072,512]{1,0:T(8,128)(2,1)} %bitcast.12, bf16[512,3072]{1,0:T(8,128)(2,1)} %bitcast.13, s32[6,2,128]{2,1,0:T(2,128)} %bitcast.16, f32[6,2,128]{2,1,0:T(2,128)} %bitcast.17), custom_call_target="tpu_custom_call" | custom-call | tf_op jit(solution)/shard_map/pallas_call | solution.py:279
  83.3 1.7 %copy.8 = bf16[1,2,24,3072]{3,2,1,0:T(8,128)(2,1)} copy(bf16[1,2,24,3072]{3,2,1,0:T(8,128)(2,1)} %bitcast.14) | data formatting | bytes 589824

commit v2 on v0

v2 whole, which is shorter than its diff:
```python
import jax
import jax.numpy as jnp
from jax import lax
from jax.experimental import pallas as pl
from jax.experimental.pallas import tpu as pltpu
from jax.sharding import PartitionSpec as P

MESH = pl.DeviceIdType.MESH
SIDE = 4
COPIES = 128
UNITS = (
    ((0, 0), (1, 0), (2, 0), (3, 0)),
    ((0, 1), (0, 3), (0, 2), (2, 3)),
    ((2, 1), (1, 1), (1, 3), (2, 2)),
    ((1, 2), (3, 1), (3, 3), (3, 2)),
)
ORDER = (
    "A0", "P2", "Q0", "B0", "P3", "A2", "A1", "F000", "O0", "F001", "F100", "C0",
    "F101", "A3", "S100", "S101", "B2", "S000", "O2", "S001", "F010", "F110", "B1", "F111",
    "S110", "O1", "S111", "F011", "S010", "B3", "R00", "N00", "O3", "S011", "R01", "N01",
    "C2", "F020", "F021", "F120", "C1", "F121", "S120", "C3", "S121", "L00", "S020", "N10",
    "R20", "N20", "F130", "L01", "F131", "S021", "N11", "R21", "N21", "S130", "T00", "S131",
    "F030", "F031", "L20", "S030", "R10", "R30", "N30", "S031", "R11", "T01", "R31", "N31",
    "L21", "T20", "L10", "L30", "L11", "L31", "T21", "T10", "D10", "T30", "D30", "T11",
    "D11", "T31", "D31", "H0", "H1",
)


def kernel(
    segments, batches,
    h_ref, wg_ref, wu_ref, wd_ref, rows_ref, gates_ref, out_ref,
    x, o, rp, ra, rb, ru, rv, fa, fb, fu, fv, fin, wg, wu, wd, act, gcol,
    local_sem, send_sem, recv_sem,
):
    f32, bf16 = jnp.float32, jnp.bfloat16
    rows, width = h_ref.shape
    shard = rows // batches
    half = width // 2
    group = SIDE * rows
    units = wg.shape[1]
    seg, me = lax.axis_index("segment"), lax.axis_index("tensor")
    core = lax.rem(me, 2)
    y = lax.rem(lax.div(me, 2), SIDE)
    z = lax.div(me, 2 * SIDE)

    def member(c, d, e):
        dy = d * (1 - c) + e * c
        dz = e * (1 - c) + d * c
        return (lax.rem(z + dz, SIDE) * SIDE + lax.rem(y + dy, SIDE)) * 2 + c

    first_up, first_down = (seg, member(core, 1, 0)), (seg, member(core, SIDE - 1, 0))
    second_up, second_down = (seg, member(core, 0, 1)), (seg, member(core, 0, SIDE - 1))
    partner = (seg, me + 1 - 2 * core)
    ahead = (lax.rem(seg + 1, segments), me)
    behind = (lax.rem(seg + segments - 1, segments), me)

    quarter = half // 2
    cols = (pl.ds(0, half), pl.ds(half, half))
    parts = tuple(pl.ds(k * quarter, quarter) for k in range(4))
    place = {owner: k for k, owner in enumerate(sum(UNITS, ()))}

    def slot(ref, f, d, e, *part):
        return ref.at[(pl.ds((f * SIDE * SIDE + place[d, e]) * rows, rows), *part)]

    def line(ref, d, *part):
        return ref.at[(pl.ds(d * rows, rows), *part)]

    used = []

    def copy(src, dst, device):
        k = len(used)
        made = pltpu.make_async_remote_copy(
            src_ref=src, dst_ref=dst, send_sem=send_sem.at[k], recv_sem=recv_sem.at[k],
            device_id=device, device_id_type=MESH,
        )
        used.append(made)
        return made

    def start(*made):
        for one in made:
            one.start()

    def arrived(*made):
        for one in made:
            one.wait_recv()

    def both(source, above, below, up, down):
        return [
            (copy(slot(x, 0, *source, cols[k]), slot(x, 0, *above, cols[k]), up),
             copy(slot(x, 0, *source, cols[1 - k]), slot(x, 0, *below, cols[1 - k]), down))
            for k in range(2)
        ]

    def onward(above, below, target, up, down):
        return (
            copy(slot(x, 0, *above, cols[0]), slot(x, 0, *target, cols[0]), up),
            copy(slot(x, 0, *below, cols[1]), slot(x, 0, *target, cols[1]), down),
        )

    p1 = both((0, 0), (3, 0), (1, 0), first_up, first_down)
    p2 = onward((3, 0), (1, 0), (2, 0), first_up, first_down)
    qa = [both((d, 0), (d, 3), (d, 1), second_up, second_down) for d in range(SIDE)]
    qb = [onward((d, 3), (d, 1), (d, 2), second_up, second_down) for d in range(SIDE)]
    over = {owner: copy(slot(x, 0, *owner), slot(x, 1, *owner), partner) for owner in place}

    def band(f, unit):
        return pl.ds((f * SIDE + unit) * group, group)

    back = [[copy(o.at[band(1, k), c], rp.at[band(0, k), c], partner) for c in cols] for k in range(SIDE)]
    pairs = [(2 * c, 2 * c + 1) for c in range(2)]

    def relayed(source, above, below, up, down):
        return [
            (copy(source(parts[k]), above(parts[c]), up), copy(source(parts[m]), below(parts[c]), down))
            for c, (k, m) in enumerate(pairs)
        ]

    def final(above, below, into_up, into_down, up, down):
        return [
            ((copy(above(parts[m]), into_up(parts[m]), up), copy(below(parts[k]), into_down(parts[k]), down)),
             (copy(above(parts[k]), into_up(parts[k]), up), copy(below(parts[m]), into_down(parts[m]), down)))
            for k, m in pairs
        ]

    term = lambda d, e: lambda part: slot(o, 0, d, e, part)
    at = lambda ref, d: lambda part: line(ref, d, part)
    r1 = [relayed(term(d, 2), at(ra, d), at(rb, d), second_up, second_down) for d in range(SIDE)]
    r2 = [final(term(d, 1), term(d, 3), at(ru, d), at(rv, d), second_up, second_down) for d in range(SIDE)]
    f1 = relayed(term(2, 0), at(fa, 0), at(fb, 0), first_up, first_down)
    f2 = final(term(1, 0), term(3, 0), at(fu, 0), at(fv, 0), first_up, first_down)
    hand = [copy(fin.at[:, c], out_ref.at[:, c], ahead) for c in cols]

    own = pltpu.make_async_copy(h_ref, slot(x, 0, 0, 0), local_sem.at[0])
    own.start()
    loads = [
        pltpu.make_async_copy(src, dst, local_sem.at[1 + k])
        for k, (src, dst) in enumerate(((wg_ref, wg), (wu_ref, wu), (wd_ref, wd)))
    ]
    start(*loads)

    barrier = pltpu.get_barrier_semaphore()
    near = (first_up, first_down, second_up, second_down, partner, ahead, behind)
    for device in near:
        pl.semaphore_signal(barrier, inc=1, device_id=device, device_id_type=MESH)

    def gates_for(f):
        for (d, e), k in place.items():
            source = member(core + f - 2 * core * f, d, e)
            token = lax.broadcasted_iota(jnp.int32, (shard, 128), 0) + source * shard
            for b in range(batches):
                total = jnp.zeros((shard, 128), f32)
                for block in range(rows_ref.shape[0]):
                    named = rows_ref[block, b : b + 1, :]
                    total += jnp.where(token == named, gates_ref[block, b : b + 1, :], 0.0)
                at = (f * SIDE * SIDE + k) * rows + b * shard
                gcol[pl.ds(at, shard), :] = jnp.broadcast_to(
                    jnp.sum(total, axis=1, keepdims=True), (shard, 128)
                )

    gates_for(0)
    pl.semaphore_wait(barrier, len(near))
    own.wait()
    start(*p1[0], *p1[1], over[0, 0])
    gates_for(1)

    step = units // 2
    wide = min(512, half)

    def first(f, unit, n):
        part = pl.ds(n * step, step)
        tokens = x[band(f, unit), :]
        g = jnp.dot(tokens, wg[:, part], preferred_element_type=f32)
        u = jnp.dot(tokens, wu[:, part], preferred_element_type=f32)
        gate = jnp.concatenate([gcol[band(f, unit), :]] * (step // 128), axis=1)
        act[f, :, part] = (g / (1.0 + jnp.exp(-g)) * u * gate).astype(bf16)

    def second(f, unit, h):
        if f == 0:
            arrived(back[unit][h])
        for n in range(half // wide):
            part = pl.ds(h * half + n * wide, wide)
            value = jnp.dot(act[f], wd[:, part], preferred_element_type=f32)
            if f == 0:
                value = value + rp[band(0, unit), part].astype(f32)
            o[band(f, unit), part] = value.astype(bf16)
        if f == 1:
            start(back[unit][h])

    def add(into, *terms):
        total = into[...].astype(f32)
        for term in terms:
            total = total + term[...].astype(f32)
        into[...] = total.astype(bf16)

    def forward(came, made):
        for one, next_one in zip(came, made):
            arrived(one)
            start(next_one)

    def side_shards(came, d, *owners):
        for one, owner in zip(came, owners):
            arrived(one)
            start(over[owner])

    def far_shard(came, owner):
        arrived(*came)
        start(over[owner])

    def send_shard(d):
        if d == 0:
            for one in p1[0]:
                one.wait_send()
        start(*qa[d][0], *qa[d][1])

    def multiply(f, unit, n):
        while loads:
            loads.pop().wait()
        if f == 1 and n == 0:
            arrived(*(over[owner] for owner in UNITS[unit]))
        first(f, unit, n)

    def relay(d, c):
        k, m = pairs[c]
        arrived(r1[d][c][0])
        add(slot(o, 0, d, 1, parts[k]), line(ra, d, parts[c]))
        start(r2[d][c][1][0])
        arrived(r1[d][c][1])
        add(slot(o, 0, d, 3, parts[m]), line(rb, d, parts[c]))
        start(r2[d][c][1][1])

    def settle(d, c):
        arrived(*r2[d][c][0], *r2[d][c][1])
        add(slot(o, 0, d, 0, cols[c]), line(ru, d, cols[c]), line(rv, d, cols[c]))
        if d == 2:
            start(*f1[c])
        elif d:
            start(f2[c][0][d // 2])

    def last_relay(d, c):
        arrived(f1[c][d // 2])
        add(slot(o, 0, d, 0, parts[pairs[c][d // 2]]), line((fa, fb)[d // 2], 0, parts[c]))
        start(f2[c][1][d // 2])

    def hand_on(c):
        arrived(*f2[c][0], *f2[c][1])
        part = cols[c]
        fin[:, part] = (
            slot(o, 0, 0, 0, part)[...].astype(f32)
            + fu[:, part].astype(f32)
            + fv[:, part].astype(f32)
            + slot(x, 0, 0, 0, part)[...].astype(f32)
        ).astype(bf16)
        start(hand[c])

    table = {
        "A": send_shard,
        "B": lambda d: forward(qa[d][0], qb[d]),
        "O": lambda d: side_shards(qa[d][1], d, (d, 3), (d, 1)),
        "C": lambda d: far_shard(qb[d], (d, 2)),
        "F": multiply,
        "S": second,
        "R": lambda d, c: start(*r1[d][c]),
        "N": lambda d, c: start(*r2[d][c][0]),
        "L": relay,
        "T": settle,
        "D": last_relay,
        "H": hand_on,
        "P": lambda k: forward(p1[0], p2) if k == 2 else far_shard(p2, (2, 0)),
        "Q": lambda k: side_shards(p1[1], 0, (3, 0), (1, 0)),
    }
    for token in ORDER:
        table[token[0]](*(int(n) for n in token[1:]))
    arrived(*hand)
    for made in used:
        if all(made is not one for one in p1[0]):
            made.wait_send()


def per_device(hidden, gate_weight, up_weight, down_weight, block_rows, slot_gate):
    batches, shard, width = hidden.shape[1:]
    rows = batches * shard
    units = gate_weight.shape[2]
    segments = lax.axis_size("segment")
    bf16 = jnp.bfloat16
    anywhere, vmem = pl.BlockSpec(memory_space=pl.ANY), pl.BlockSpec(memory_space=pltpu.VMEM)

    def body(*refs):
        kernel(segments, batches, *refs)

    handed = pl.pallas_call(
        body,
        out_shape=pltpu.VMEM((rows, width), bf16),
        in_specs=[anywhere] * 4 + [vmem] * 2,
        out_specs=anywhere,
        scratch_shapes=[
            pltpu.VMEM((32 * rows, width), bf16),
            pltpu.VMEM((32 * rows, width), bf16),
            pltpu.VMEM((16 * rows, width), bf16),
            pltpu.VMEM((4 * rows, width // 2), bf16),
            pltpu.VMEM((4 * rows, width // 2), bf16),
            pltpu.VMEM((4 * rows, width), bf16),
            pltpu.VMEM((4 * rows, width), bf16),
            pltpu.VMEM((rows, width // 2), bf16),
            pltpu.VMEM((rows, width // 2), bf16),
            pltpu.VMEM((rows, width), bf16),
            pltpu.VMEM((rows, width), bf16),
            pltpu.VMEM((rows, width), bf16),
            pltpu.VMEM((width, units), bf16),
            pltpu.VMEM((width, units), bf16),
            pltpu.VMEM((units, width), bf16),
            pltpu.VMEM((2, 4 * rows, units), bf16),
            pltpu.VMEM((32 * rows, 128), jnp.float32),
            pltpu.SemaphoreType.DMA((4,)),
            pltpu.SemaphoreType.DMA((COPIES,)),
            pltpu.SemaphoreType.DMA((COPIES,)),
        ],
        compiler_params=pltpu.CompilerParams(
            collective_id=0, has_side_effects=True, vmem_limit_bytes=60 * 1024 * 1024
        ),
    )(
        hidden.reshape(rows, width),
        gate_weight[0],
        up_weight[0],
        down_weight[0],
        block_rows[0].transpose(1, 0, 2),
        slot_gate[0].transpose(1, 0, 2),
    )
    return handed.reshape(hidden.shape)


def solution(mesh):
    return jax.shard_map(
        per_device,
        mesh=mesh,
        in_specs=(
            P("segment", None, "tensor", None),
            P("segment", None, "tensor"),
            P("segment", None, "tensor"),
            P("segment", "tensor", None),
            P("segment", None, None, None),
            P("segment", None, None, None),
        ),
        out_specs=P("segment", None, "tensor", None),
        check_vma=False,
    )
```

time: 207 us -> 73.2 us (0.35)
  waiting for transfers between devices: 161 us -> 0 us
  Pallas kernels: 0 us -> 71.6 us
  matrix products: 26.9 us -> 0 us
  between operations: 13.4 us -> 0.01 us
  other arithmetic: 2.53 us -> 0 us
    reduce_scatter x1 -> x0, waiting for transfers between devices: 95.3 us -> none  [per_device(): lax.psum_scatter(part.astype(jnp.bfloat16), 'tensor', scatter_dimension=0...]
    pallas_call x0 -> x1, Pallas kernels: none -> 71.6 us  [per_device(): pl.pallas_call(body, out_shape=pltpu.VMEM((rows, width), bf16), in_specs=...]
    all_gather x1 -> x0, waiting for transfers between devices: 58.4 us -> none  [per_device(): gathered = lax.all_gather(own, 'tensor', axis=0, tiled=True)]
    dot_general x2 -> x0, matrix products: 26.9 us -> none  [the longest x1 16.3 us: per_device(): jnp.dot(hidden_act, down_weight[0], preferred_element_type=jnp.float32)]
    ppermute x1 -> x0, waiting for transfers between devices: 6.69 us -> none  [from_behind(): return lax.ppermute(value, axis, pairs)]
  transfers between devices with their start and end apart: 3 -> 0, of which waited for: 3 -> 0; matrix products, arithmetic and copies ran while one was open for 1% -> 0% of each run, Pallas kernels for 0% -> 0%
where the time goes in v2:
time: 73.2 us; the launch traced here: 72.3 us
  Pallas kernels  71.6 us (98%)
    pallas_call x1, Pallas kernels, per_device(): pl.pallas_call(body, out_shape=pltpu.VMEM((rows, width), bf16), in_specs=...  71.6 us

profile of v2, /device:TPU:0, one launch (start us, length us, event | category | flops | bytes accessed | tf_op | source)
XLA Modules:
  0.0 72.3 jit_solution(7819588049377536182)
XLA Ops:
  0.0 71.6 %shard_map.64 = bf16[48,3072]{1,0:T(8,128)(2,1)S(1)} custom-call(bf16[48,3072]{1,0:T(8,128)(2,1)} %bitcast.15, bf16[3072,512]{1,0:T(8,128)(2,1)} %bitcast.12, bf16[3072,512]{1,0:T(8,128)(2,1)} %bitcast.13, bf16[512,3072]{1,0:T(8,128)(2,1)} %bitcast.14, s32[6,2,128]{2,1,0:T(2,128)} %bitcast.16, f32[6,2,128]{2,1,0:T(2,128)} %bitcast.17), custom_call_target="tpu_custom_call" | custom-call | tf_op jit(solution)/shard_map/pallas_call | solution.py:290
  71.6 0.7 copy.8

commit v3 on v2

--- a/solution.py
+++ b/solution.py
@@ -9,27 +9,26 @@
 SIDE = 4
 COPIES = 128
 UNITS = (
-    ((0, 0), (1, 0), (2, 0), (3, 0)),
-    ((0, 1), (0, 3), (0, 2), (2, 3)),
-    ((2, 1), (1, 1), (1, 3), (2, 2)),
+    ((0, 0), (1, 0), (2, 0), (0, 2)),
+    ((0, 1), (2, 1), (0, 3), (2, 3)),
+    ((3, 0), (1, 1), (1, 3), (2, 2)),
     ((1, 2), (3, 1), (3, 3), (3, 2)),
 )
 ORDER = (
-    "A0", "P2", "Q0", "B0", "P3", "A2", "A1", "F000", "O0", "F001", "F100", "C0",
-    "F101", "A3", "S100", "S101", "B2", "S000", "O2", "S001", "F010", "F110", "B1", "F111",
-    "S110", "O1", "S111", "F011", "S010", "B3", "R00", "N00", "O3", "S011", "R01", "N01",
-    "C2", "F020", "F021", "F120", "C1", "F121", "S120", "C3", "S121", "L00", "S020", "N10",
-    "R20", "N20", "F130", "L01", "F131", "S021", "N11", "R21", "N21", "S130", "T00", "S131",
-    "F030", "F031", "L20", "S030", "R10", "R30", "N30", "S031", "R11", "T01", "R31", "N31",
-    "L21", "T20", "L10", "L30", "L11", "L31", "T21", "T10", "D10", "T30", "D30", "T11",
-    "D11", "T31", "D31", "H0", "H1",
+    "A0", "P2", "Q0", "B0", "P3", "A2", "O0", "A1", "C0", "F000", "F100", "B2",
+    "S100", "S101", "O2", "A3", "B1", "S000", "O1", "S001", "F110", "C2", "S110", "S111",
+    "R00", "F010", "B3", "F120", "O3", "R01", "S010", "C1", "N20", "S011", "S120", "N21",
+    "N00", "L00", "S121", "F020", "C3", "N01", "L01", "S020", "R20", "S021", "F130", "R21",
+    "N10", "S130", "N11", "S131", "T00", "F030", "T01", "L20", "L21", "S030", "R10", "S031",
+    "R30", "N30", "T20", "T21", "R11", "L10", "L30", "R31", "N31", "L11", "T10", "D10",
+    "T30", "D30", "L31", "T11", "D11", "T31", "D31", "H0", "H1",
 )
 
 
 def kernel(
     segments, batches,
-    h_ref, wg_ref, wu_ref, wd_ref, rows_ref, gates_ref, out_ref,
-    x, o, rp, ra, rb, ru, rv, fa, fb, fu, fv, fin, wg, wu, wd, act, gcol,
+    h_ref, wg_ref, wu_ref, wd_ref, rows_any, gates_any, out_ref,
+    x, o, rp, ra, rb, ru, rv, fa, fb, fu, fv, fin, wg, wu, wd, act, gcol, rows_ref, gates_ref,
     local_sem, send_sem, recv_sem,
 ):
     f32, bf16 = jnp.float32, jnp.bfloat16
@@ -54,9 +53,13 @@
     ahead = (lax.rem(seg + 1, segments), me)
     behind = (lax.rem(seg + segments - 1, segments), me)
 
-    quarter = half // 2
     cols = (pl.ds(0, half), pl.ds(half, half))
-    parts = tuple(pl.ds(k * quarter, quarter) for k in range(4))
+    narrow = width // 4
+    groups = (pl.ds(0, width - narrow), pl.ds(width - narrow, narrow))
+    parts = tuple(
+        pl.ds(g.start + k * (g.size // 2), g.size // 2) for g in groups for k in range(2)
+    )
+    lanes = (pl.ds(0, half - narrow // 2), pl.ds(half - narrow // 2, narrow // 2))
     place = {owner: k for k, owner in enumerate(sum(UNITS, ()))}
 
     def slot(ref, f, d, e, *part):
@@ -106,12 +109,12 @@
     def band(f, unit):
         return pl.ds((f * SIDE + unit) * group, group)
 
-    back = [[copy(o.at[band(1, k), c], rp.at[band(0, k), c], partner) for c in cols] for k in range(SIDE)]
+    back = [[copy(o.at[band(1, k), c], rp.at[band(0, k), c], partner) for c in groups] for k in range(SIDE)]
     pairs = [(2 * c, 2 * c + 1) for c in range(2)]
 
     def relayed(source, above, below, up, down):
         return [
-            (copy(source(parts[k]), above(parts[c]), up), copy(source(parts[m]), below(parts[c]), down))
+            (copy(source(parts[k]), above(lanes[c]), up), copy(source(parts[m]), below(lanes[c]), down))
             for c, (k, m) in enumerate(pairs)
         ]
 
@@ -128,20 +131,24 @@
     r2 = [final(term(d, 1), term(d, 3), at(ru, d), at(rv, d), second_up, second_down) for d in range(SIDE)]
     f1 = relayed(term(2, 0), at(fa, 0), at(fb, 0), first_up, first_down)
     f2 = final(term(1, 0), term(3, 0), at(fu, 0), at(fv, 0), first_up, first_down)
-    hand = [copy(fin.at[:, c], out_ref.at[:, c], ahead) for c in cols]
-
-    own = pltpu.make_async_copy(h_ref, slot(x, 0, 0, 0), local_sem.at[0])
-    own.start()
-    loads = [
-        pltpu.make_async_copy(src, dst, local_sem.at[1 + k])
-        for k, (src, dst) in enumerate(((wg_ref, wg), (wu_ref, wu), (wd_ref, wd)))
-    ]
-    start(*loads)
+    hand = [copy(fin.at[:, c], out_ref.at[:, c], ahead) for c in groups]
 
     barrier = pltpu.get_barrier_semaphore()
     near = (first_up, first_down, second_up, second_down, partner, ahead, behind)
     for device in near:
         pl.semaphore_signal(barrier, inc=1, device_id=device, device_id_type=MESH)
+    own, *loads = [
+        pltpu.make_async_copy(src, dst, local_sem.at[k])
+        for k, (src, dst) in enumerate(
+            (
+                (h_ref, slot(x, 0, 0, 0)), (rows_any, rows_ref), (gates_any, gates_ref),
+                (wg_ref, wg), (wu_ref, wu), (wd_ref, wd),
+            )
+        )
+    ]
+    start(own, *loads)
+    for _ in range(2):
+        loads.pop(0).wait()
 
     def gates_for(f):
         for (d, e), k in place.items():
@@ -164,21 +171,21 @@
     gates_for(1)
 
     step = units // 2
-    wide = min(512, half)
-
-    def first(f, unit, n):
-        part = pl.ds(n * step, step)
-        tokens = x[band(f, unit), :]
-        g = jnp.dot(tokens, wg[:, part], preferred_element_type=f32)
-        u = jnp.dot(tokens, wu[:, part], preferred_element_type=f32)
-        gate = jnp.concatenate([gcol[band(f, unit), :]] * (step // 128), axis=1)
-        act[f, :, part] = (g / (1.0 + jnp.exp(-g)) * u * gate).astype(bf16)
+
+    def first(f, unit, _):
+        for n in range(2):
+            part = pl.ds(n * step, step)
+            tokens = x[band(f, unit), :]
+            g = jnp.dot(tokens, wg[:, part], preferred_element_type=f32)
+            u = jnp.dot(tokens, wu[:, part], preferred_element_type=f32)
+            gate = jnp.concatenate([gcol[band(f, unit), :]] * (step // 128), axis=1)
+            act[f, :, part] = (g / (1.0 + jnp.exp(-g)) * u * gate).astype(bf16)
 
     def second(f, unit, h):
         if f == 0:
             arrived(back[unit][h])
-        for n in range(half // wide):
-            part = pl.ds(h * half + n * wide, wide)
+        for n in range(groups[h].size // narrow):
+            part = pl.ds(groups[h].start + n * narrow, narrow)
             value = jnp.dot(act[f], wd[:, part], preferred_element_type=f32)
             if f == 0:
                 value = value + rp[band(0, unit), part].astype(f32)
@@ -222,15 +229,15 @@
     def relay(d, c):
         k, m = pairs[c]
         arrived(r1[d][c][0])
-        add(slot(o, 0, d, 1, parts[k]), line(ra, d, parts[c]))
+        add(slot(o, 0, d, 1, parts[k]), line(ra, d, lanes[c]))
         start(r2[d][c][1][0])
         arrived(r1[d][c][1])
-        add(slot(o, 0, d, 3, parts[m]), line(rb, d, parts[c]))
+        add(slot(o, 0, d, 3, parts[m]), line(rb, d, lanes[c]))
         start(r2[d][c][1][1])
 
     def settle(d, c):
         arrived(*r2[d][c][0], *r2[d][c][1])
-        add(slot(o, 0, d, 0, cols[c]), line(ru, d, cols[c]), line(rv, d, cols[c]))
+        add(slot(o, 0, d, 0, groups[c]), line(ru, d, groups[c]), line(rv, d, groups[c]))
         if d == 2:
             start(*f1[c])
         elif d:
@@ -238,12 +245,12 @@
 
     def last_relay(d, c):
         arrived(f1[c][d // 2])
-        add(slot(o, 0, d, 0, parts[pairs[c][d // 2]]), line((fa, fb)[d // 2], 0, parts[c]))
+        add(slot(o, 0, d, 0, parts[pairs[c][d // 2]]), line((fa, fb)[d // 2], 0, lanes[c]))
         start(f2[c][1][d // 2])
 
     def hand_on(c):
         arrived(*f2[c][0], *f2[c][1])
-        part = cols[c]
+        part = groups[c]
         fin[:, part] = (
             slot(o, 0, 0, 0, part)[...].astype(f32)
             + fu[:, part].astype(f32)
@@ -270,10 +277,12 @@
     }
     for token in ORDER:
         table[token[0]](*(int(n) for n in token[1:]))
+    for made in used:
+        if all(made is not one for one in (*p1[0], *hand)):
+            made.wait_send()
     arrived(*hand)
-    for made in used:
-        if all(made is not one for one in p1[0]):
-            made.wait_send()
+    for made in hand:
+        made.wait_send()
 
 
 def per_device(hidden, gate_weight, up_weight, down_weight, block_rows, slot_gate):
@@ -282,7 +291,8 @@
     units = gate_weight.shape[2]
     segments = lax.axis_size("segment")
     bf16 = jnp.bfloat16
-    anywhere, vmem = pl.BlockSpec(memory_space=pl.ANY), pl.BlockSpec(memory_space=pltpu.VMEM)
+    anywhere = pl.BlockSpec(memory_space=pl.ANY)
+    tables = block_rows[0].transpose(1, 0, 2), slot_gate[0].transpose(1, 0, 2)
 
     def body(*refs):
         kernel(segments, batches, *refs)
@@ -290,7 +300,7 @@
     handed = pl.pallas_call(
         body,
         out_shape=pltpu.VMEM((rows, width), bf16),
-        in_specs=[anywhere] * 4 + [vmem] * 2,
+        in_specs=[anywhere] * 6,
         out_specs=anywhere,
         scratch_shapes=[
             pltpu.VMEM((32 * rows, width), bf16),
@@ -310,7 +320,8 @@
             pltpu.VMEM((units, width), bf16),
             pltpu.VMEM((2, 4 * rows, units), bf16),
             pltpu.VMEM((32 * rows, 128), jnp.float32),
-            pltpu.SemaphoreType.DMA((4,)),
+            *(pltpu.VMEM(table.shape, table.dtype) for table in tables),
+            pltpu.SemaphoreType.DMA((6,)),
             pltpu.SemaphoreType.DMA((COPIES,)),
             pltpu.SemaphoreType.DMA((COPIES,)),
         ],
@@ -322,8 +333,7 @@
         gate_weight[0],
         up_weight[0],
         down_weight[0],
-        block_rows[0].transpose(1, 0, 2),
-        slot_gate[0].transpose(1, 0, 2),
+        *tables,
     )
     return handed.reshape(hidden.shape)
 

time: 73.2 us -> 71.2 us (0.973); the launches traced: 72.3 us -> 71.1 us
  Pallas kernels: 71.6 us -> 70.4 us
    pallas_call x1, Pallas kernels: 71.6 us -> 70.4 us  [per_device(): pl.pallas_call(body, out_shape=pltpu.VMEM((rows, width), bf16), in_specs=...]
where the time goes in v3:
time: 71.2 us; the launch traced here: 71.1 us
  Pallas kernels  70.4 us (99%)
  local copies, waits for them, and re-layouts  0.72 us (1%)
    pallas_call x1, Pallas kernels, per_device(): pl.pallas_call(body, out_shape=pltpu.VMEM((rows, width), bf16), in_specs=...  70.4 us

profile of v3, /device:TPU:0, one launch (start us, length us, event | category | flops | bytes accessed | tf_op | source)
XLA Modules:
  0.0 71.1 jit_solution(14228997324599495193)
XLA Ops:
  0.0 70.4 %shard_map.64 = bf16[48,3072]{1,0:T(8,128)(2,1)S(1)} custom-call(bf16[48,3072]{1,0:T(8,128)(2,1)} %bitcast.15, bf16[3072,512]{1,0:T(8,128)(2,1)} %bitcast.12, bf16[3072,512]{1,0:T(8,128)(2,1)} %bitcast.13, bf16[512,3072]{1,0:T(8,128)(2,1)} %bitcast.14, s32[6,2,128]{2,1,0:T(2,128)} %bitcast.16, f32[6,2,128]{2,1,0:T(2,128)} %bitcast.17), custom_call_target="tpu_custom_call" | custom-call | tf_op jit(solution)/shard_map/pallas_call | solution.py:300
  70.4 0.7 %copy.8 = bf16[1,2,24,3072]{3,2,1,0:T(8,128)(2,1)} copy(bf16[1,2,24,3072]{3,2,1,0:T(8,128)(2,1)S(1)} %bitcast.11) | data formatting | bytes 589824

commit v4 on v3

v4 whole, which is shorter than its diff:
```python
import math

import jax
import jax.numpy as jnp
from jax import lax
from jax.experimental import pallas as pl
from jax.experimental.pallas import tpu as pltpu
from jax.sharding import PartitionSpec as P

MESH = pl.DeviceIdType.MESH
SIDE = 4
SENDERS, RECEIVERS = 13, 63
UNITS = (
    ((1, 0), (0, 0), (3, 0)),
    ((0, 3), (0, 2), (0, 1)),
    ((1, 3), (1, 1), (2, 1)),
    ((2, 3), (1, 2), (2, 2)),
    ((3, 1), (3, 2), (2, 0), (3, 3)),
)
ORDER = (
    "A0", "P2", "B0", "Q0", "A1", "O0", "F100", "S100", "P3", "A2", "F000", "C0",
    "B1", "S101", "F110", "S111", "B2", "S110", "A3", "S000", "O1", "O2", "S001", "F010",
    "C1", "S011", "S010", "R00", "F120", "C2", "S121", "B3", "R01", "S120", "N00", "F130",
    "S131", "S130", "L00", "F020", "S021", "O3", "N01", "N11", "S020", "N10", "C3", "F030",
    "S031", "L01", "R11", "S030", "R20", "N20", "R21", "T00", "N21", "F140", "S141", "R10",
    "S140", "F040", "L20", "S041", "N31", "L21", "R31", "S040", "R30", "N30", "L11", "L10",
    "L31", "T21", "L30", "T01", "T11", "T20", "T31", "T10", "D31", "D11", "T30", "D10",
    "D30", "H1", "H0",
)


def kernel(
    segments, batches,
    h_ref, wg_ref, wu_ref, wd_ref, rows_any, gates_any, out_ref,
    x, o, rp, far, near_by, fa, fb, ends, fin, wg, wu, wd, act, gcol, rows_ref, gates_ref,
    local_sem, send_sem, recv_sem,
):
    f32, bf16 = jnp.float32, jnp.bfloat16
    rows, width = h_ref.shape
    shard = rows // batches
    half = width // 2
    units = wg.shape[1]
    seg, me = lax.axis_index("segment"), lax.axis_index("tensor")
    core = lax.rem(me, 2)
    y = lax.rem(lax.div(me, 2), SIDE)
    z = lax.div(me, 2 * SIDE)

    def member(c, d, e):
        dy = d * (1 - c) + e * c
        dz = e * (1 - c) + d * c
        return (lax.rem(z + dz, SIDE) * SIDE + lax.rem(y + dy, SIDE)) * 2 + c

    first_up, first_down = (seg, member(core, 1, 0)), (seg, member(core, SIDE - 1, 0))
    second_up, second_down = (seg, member(core, 0, 1)), (seg, member(core, 0, SIDE - 1))
    partner = (seg, me + 1 - 2 * core)
    ahead = (lax.rem(seg + 1, segments), me)
    behind = (lax.rem(seg + segments - 1, segments), me)

    cols = (pl.ds(0, half), pl.ds(half, half))
    narrow = width // 4
    groups = (pl.ds(0, width - narrow), pl.ds(width - narrow, narrow))
    parts = tuple(
        pl.ds(g.start + k * (g.size // 2), g.size // 2) for g in groups for k in range(2)
    )
    lanes = (pl.ds(0, half - narrow // 2), pl.ds(half - narrow // 2, narrow // 2))
    place = {owner: k for k, owner in enumerate(sum(UNITS, ()))}

    def slot(ref, f, d, e, *part):
        return ref.at[(pl.ds((f * SIDE * SIDE + place[d, e]) * rows, rows), *part)]

    def line(ref, d, *part):
        return ref.at[(pl.ds(d * rows, rows), *part)]

    senders, receivers, sent = {}, {}, {}

    def copy(src, dst, device, kind, *key):
        made = pltpu.make_async_remote_copy(
            src_ref=src, dst_ref=dst,
            send_sem=send_sem.at[senders.setdefault(kind, len(senders))],
            recv_sem=recv_sem.at[receivers.setdefault((kind, *key), len(receivers))],
            device_id=device, device_id_type=MESH,
        )
        sent.setdefault(kind, []).append(src.shape)
        return made

    def start(*made):
        for one in made:
            one.start()

    def arrived(whole, kind, *key):
        pltpu.make_async_remote_copy(
            src_ref=whole, dst_ref=whole, send_sem=send_sem.at[senders[kind]],
            recv_sem=recv_sem.at[receivers[kind, *key]], device_id=partner, device_id_type=MESH,
        ).wait_recv()

    def all_sent(kind):
        count = sum(math.prod(shape) for shape in sent[kind]) // width
        whole = x.at[pl.ds(0, count)]
        pltpu.make_async_remote_copy(
            src_ref=whole, dst_ref=whole, send_sem=send_sem.at[senders[kind]],
            recv_sem=recv_sem.at[0], device_id=partner, device_id_type=MESH,
        ).wait_send()

    def two(ref, d, *part):
        return ref.at[(pl.ds(2 * d * rows, 2 * rows), *part)]

    def shard_of(owner, *part):
        return slot(x, 0, *owner, *part) if any(owner) else h_ref.at[(slice(None), *part)]

    def both(source, above, below, up, down, kind, d):
        return [
            (copy(shard_of(source, cols[k]), slot(x, 0, *above, cols[k]), up, kind + str(k), d, 0),
             copy(shard_of(source, cols[1 - k]), slot(x, 0, *below, cols[1 - k]), down, kind + str(k), d, 1))
            for k in range(2)
        ]

    def onward(above, below, target, up, down, kind, d):
        return (
            copy(slot(x, 0, *above, cols[0]), slot(x, 0, *target, cols[0]), up, kind, d),
            copy(slot(x, 0, *below, cols[1]), slot(x, 0, *target, cols[1]), down, kind, d),
        )

    unit_of = {owner: k for k, unit in enumerate(UNITS) for owner in unit}
    p1 = both((0, 0), (3, 0), (1, 0), first_up, first_down, "p", 0)
    p2 = onward((3, 0), (1, 0), (2, 0), first_up, first_down, "p2", 0)
    qa = [both((d, 0), (d, 3), (d, 1), second_up, second_down, "q", d) for d in range(SIDE)]
    qb = [onward((d, 3), (d, 1), (d, 2), second_up, second_down, "q2", d) for d in range(SIDE)]
    over = {owner: copy(shard_of(owner), slot(x, 1, *owner), partner, "over", k) for owner, k in unit_of.items()}

    begin = [sum(len(unit) for unit in UNITS[:k]) for k in range(len(UNITS))]

    def band(f, unit):
        return pl.ds((f * SIDE * SIDE + begin[unit]) * rows, len(UNITS[unit]) * rows)

    back = [
        [copy(o.at[band(1, k), g], rp.at[band(0, k), g], partner, "back", k, c) for c, g in enumerate(groups)]
        for k in range(len(UNITS))
    ]
    pairs = [(2 * c, 2 * c + 1) for c in range(2)]

    def relayed(source, above, below, up, down, kind, d, apart):
        return [
            (copy(source(parts[k]), above(lanes[c]), up, kind, d, c),
             copy(source(parts[m]), below(lanes[c]), down, kind, d, c + 2 * apart))
            for c, (k, m) in enumerate(pairs)
        ]

    def final(above, below, into, d, up, down, kind):
        into_up, into_down = at(into, 2 * d), at(into, 2 * d + 1)
        return [
            ((copy(above(parts[m]), into_up(parts[m]), up, kind, d, c),
              copy(below(parts[k]), into_down(parts[k]), down, kind, d, c)),
             (copy(above(parts[k]), into_up(parts[k]), up, kind, d, c),
              copy(below(parts[m]), into_down(parts[m]), down, kind, d, c)))
            for c, (k, m) in enumerate(pairs)
        ]

    term = lambda d, e: lambda part: slot(o, 0, d, e, part)
    at = lambda ref, d: lambda part: line(ref, d, part)
    r1 = [
        relayed(term(d, 2), at(far, 2 * d), at(far, 2 * d + 1), second_up, second_down, "r1", d, 0)
        for d in range(SIDE)
    ]
    r2 = [final(term(d, 1), term(d, 3), near_by, d, second_up, second_down, "r2") for d in range(SIDE)]
    f1 = relayed(term(2, 0), at(fa, 0), at(fb, 0), first_up, first_down, "f1", 0, 1)
    f2 = final(term(1, 0), term(3, 0), ends, 0, first_up, first_down, "f2")
    hand = [copy(fin.at[:, g], out_ref.at[:, g], ahead, "hand") for g in groups]

    barrier = pltpu.get_barrier_semaphore()
    near = (first_up, first_down, second_up, second_down, partner, ahead, behind)
    for device in near:
        pl.semaphore_signal(barrier, inc=1, device_id=device, device_id_type=MESH)
    own, *loads = [
        pltpu.make_async_copy(src, dst, local_sem.at[k])
        for k, (src, dst) in enumerate(
            (
                (h_ref, slot(x, 0, 0, 0)), (rows_any, rows_ref), (gates_any, gates_ref),
                (wg_ref, wg), (wu_ref, wu), (wd_ref, wd),
            )
        )
    ]
    start(own, *loads)

    def gates_for(f):
        for (d, e), k in place.items():
            source = member(core + f - 2 * core * f, d, e)
            token = lax.broadcasted_iota(jnp.int32, (shard, 128), 0) + source * shard
            for b in range(batches):
                total = jnp.zeros((shard, 128), f32)
                for block in range(rows_ref.shape[0]):
                    named = rows_ref[block, b : b + 1, :]
                    total += jnp.where(token == named, gates_ref[block, b : b + 1, :], 0.0)
                at = (f * SIDE * SIDE + k) * rows + b * shard
                gcol[pl.ds(at, shard), :] = jnp.broadcast_to(
                    jnp.sum(total, axis=1, keepdims=True), (shard, 128)
                )

    pl.semaphore_wait(barrier, len(near))
    start(*p1[0], *p1[1], over[0, 0])
    for _ in range(2):
        loads.pop(0).wait()
    gates_for(0)
    gates_for(1)
    own.wait()

    step = units // 2

    def first(f, unit, _):
        for n in range(2):
            part = pl.ds(n * step, step)
            tokens = x[band(f, unit), :]
            g = jnp.dot(tokens, wg[:, part], preferred_element_type=f32)
            u = jnp.dot(tokens, wu[:, part], preferred_element_type=f32)
            gate = jnp.concatenate([gcol[band(f, unit), :]] * (step // 128), axis=1)
            act[f, : tokens.shape[0], part] = (g / (1.0 + jnp.exp(-g)) * u * gate).astype(bf16)

    def second(f, unit, h):
        if f == 0:
            arrived(rp.at[band(0, unit), groups[h]], "back", unit, h)
        for n in range(groups[h].size // narrow):
            part = pl.ds(groups[h].start + n * narrow, narrow)
            value = jnp.dot(act[f, : len(UNITS[unit]) * rows, :], wd[:, part], preferred_element_type=f32)
            if f == 0:
                value = value + rp[band(0, unit), part].astype(f32)
            o[band(f, unit), part] = value.astype(bf16)
        if f == 1:
            start(back[unit][h])

    def add(into, *terms):
        total = into[...].astype(f32)
        for term in terms:
            total = total + term[...].astype(f32)
        into[...] = total.astype(bf16)

    def forward(kind, d, made, *owners):
        for k, owner in enumerate(owners):
            arrived(slot(x, 0, *owner, cols[k]), kind, d, k)
            start(made[k])

    def side_shards(kind, d, *owners):
        for k, owner in enumerate(owners):
            arrived(slot(x, 0, *owner, cols[1 - k]), kind, d, k)
            start(over[owner])

    def far_shard(kind, d, owner):
        arrived(slot(x, 0, *owner), kind, d)
        start(over[owner])

    def send_shard(d):
        if d == 0:
            all_sent("p0")
        start(*qa[d][0], *qa[d][1])

    def multiply(f, unit, n):
        while loads:
            loads.pop().wait()
        if f == 1 and n == 0:
            arrived(x.at[band(1, unit)], "over", unit)
        first(f, unit, n)

    def relay(d, c):
        k, m = pairs[c]
        arrived(two(far, d, lanes[c]), "r1", d, c)
        add(slot(o, 0, d, 1, parts[k]), line(far, 2 * d, lanes[c]))
        start(r2[d][c][1][0])
        add(slot(o, 0, d, 3, parts[m]), line(far, 2 * d + 1, lanes[c]))
        start(r2[d][c][1][1])

    def settle(d, c):
        arrived(two(near_by, d, groups[c]), "r2", d, c)
        add(slot(o, 0, d, 0, groups[c]), line(near_by, 2 * d, groups[c]), line(near_by, 2 * d + 1, groups[c]))
        if d == 2:
            start(*f1[c])
        elif d:
            start(f2[c][0][d // 2])

    def last_relay(d, c):
        side = d // 2
        came = line((fa, fb)[side], 0, lanes[c])
        arrived(came, "f1", 0, c + 2 * side)
        add(slot(o, 0, d, 0, parts[pairs[c][side]]), came)
        start(f2[c][1][side])

    def hand_on(c):
        part = groups[c]
        arrived(two(ends, 0, part), "f2", 0, c)
        fin[:, part] = (
            slot(o, 0, 0, 0, part)[...].astype(f32)
            + line(ends, 0, part)[...].astype(f32)
            + line(ends, 1, part)[...].astype(f32)
            + slot(x, 0, 0, 0, part)[...].astype(f32)
        ).astype(bf16)
        start(hand[c])

    table = {
        "A": send_shard,
        "B": lambda d: forward("q0", d, qb[d], (d, 3), (d, 1)),
        "O": lambda d: side_shards("q1", d, (d, 3), (d, 1)),
        "C": lambda d: far_shard("q2", d, (d, 2)),
        "F": multiply,
        "S": second,
        "R": lambda d, c: start(*r1[d][c]),
        "N": lambda d, c: start(*r2[d][c][0]),
        "L": relay,
        "T": settle,
        "D": last_relay,
        "H": hand_on,
        "P": lambda k: forward("p0", 0, p2, (3, 0), (1, 0)) if k == 2 else far_shard("p2", 0, (2, 0)),
        "Q": lambda k: side_shards("p1", 0, (3, 0), (1, 0)),
    }
    for token in ORDER:
        table[token[0]](*(int(n) for n in token[1:]))
    for kind in sent:
        if kind not in ("p0", "hand"):
            all_sent(kind)
    arrived(out_ref, "hand")
    all_sent("hand")
    assert len(senders) <= SENDERS and len(receivers) <= RECEIVERS


def per_device(hidden, gate_weight, up_weight, down_weight, block_rows, slot_gate):
    batches, shard, width = hidden.shape[1:]
    rows = batches * shard
    units = gate_weight.shape[2]
    segments = lax.axis_size("segment")
    bf16 = jnp.bfloat16
    anywhere = pl.BlockSpec(memory_space=pl.ANY)
    tables = block_rows[0].transpose(1, 0, 2), slot_gate[0].transpose(1, 0, 2)

    def body(*refs):
        kernel(segments, batches, *refs)

    handed = pl.pallas_call(
        body,
        out_shape=pltpu.VMEM((rows, width), bf16),
        in_specs=[anywhere] * 6,
        out_specs=anywhere,
        scratch_shapes=[
            pltpu.VMEM((32 * rows, width), bf16),
            pltpu.VMEM((32 * rows, width), bf16),
            pltpu.VMEM((16 * rows, width), bf16),
            pltpu.VMEM((8 * rows, width // 2), bf16),
            pltpu.VMEM((8 * rows, width), bf16),
            pltpu.VMEM((rows, width // 2), bf16),
            pltpu.VMEM((rows, width // 2), bf16),
            pltpu.VMEM((2 * rows, width), bf16),
            pltpu.VMEM((rows, width), bf16),
            pltpu.VMEM((width, units), bf16),
            pltpu.VMEM((width, units), bf16),
            pltpu.VMEM((units, width), bf16),
            pltpu.VMEM((2, max(map(len, UNITS)) * rows, units), bf16),
            pltpu.VMEM((32 * rows, 128), jnp.float32),
            *(pltpu.VMEM(table.shape, table.dtype) for table in tables),
            pltpu.SemaphoreType.DMA((6,)),
            pltpu.SemaphoreType.DMA((SENDERS,)),
            pltpu.SemaphoreType.DMA((RECEIVERS,)),
        ],
        compiler_params=pltpu.CompilerParams(
            collective_id=0, has_side_effects=True, vmem_limit_bytes=60 * 1024 * 1024
        ),
    )(
        hidden.reshape(rows, width),
        gate_weight[0],
        up_weight[0],
        down_weight[0],
        *tables,
    )
    return handed.reshape(hidden.shape)


def solution(mesh):
    return jax.shard_map(
        per_device,
        mesh=mesh,
        in_specs=(
            P("segment", None, "tensor", None),
            P("segment", None, "tensor"),
            P("segment", None, "tensor"),
            P("segment", "tensor", None),
            P("segment", None, None, None),
            P("segment", None, None, None),
        ),
        out_specs=P("segment", None, "tensor", None),
        check_vma=False,
    )
```

time: 71.2 us -> 68 us (0.955)
  Pallas kernels: 70.4 us -> 67.2 us
    pallas_call x1, Pallas kernels: 70.4 us -> 67.2 us  [per_device(): pl.pallas_call(body, out_shape=pltpu.VMEM((rows, width), bf16), in_specs=...]
where the time goes in v4:
time: 68 us; the launch traced here: 67.9 us
  Pallas kernels  67.2 us (99%)
  local copies, waits for them, and re-layouts  0.72 us (1%)
    pallas_call x1, Pallas kernels, per_device(): pl.pallas_call(body, out_shape=pltpu.VMEM((rows, width), bf16), in_specs=...  67.2 us

profile of v4, /device:TPU:0, one launch (start us, length us, event | category | flops | bytes accessed | tf_op | source)
XLA Modules:
  0.0 67.9 jit_solution(14096814358494306020)
XLA Ops:
  0.0 67.2 %shard_map.64 = bf16[48,3072]{1,0:T(8,128)(2,1)S(1)} custom-call(bf16[48,3072]{1,0:T(8,128)(2,1)} %bitcast.15, bf16[3072,512]{1,0:T(8,128)(2,1)} %bitcast.12, bf16[3072,512]{1,0:T(8,128)(2,1)} %bitcast.13, bf16[512,3072]{1,0:T(8,128)(2,1)} %bitcast.14, s32[6,2,128]{2,1,0:T(2,128)} %bitcast.16, f32[6,2,128]{2,1,0:T(2,128)} %bitcast.17), custom_call_target="tpu_custom_call" | custom-call | tf_op jit(solution)/shard_map/pallas_call | solution.py:333
  67.2 0.7 %copy.8 = bf16[1,2,24,3072]{3,2,1,0:T(8,128)(2,1)} copy(bf16[1,2,24,3072]{3,2,1,0:T(8,128)(2,1)S(1)} %bitcast.11) | data formatting | bytes 589824

commit v5 on v4

--- a/solution.py
+++ b/solution.py
@@ -10,22 +10,23 @@
 MESH = pl.DeviceIdType.MESH
 SIDE = 4
 SENDERS, RECEIVERS = 13, 63
+NARROW = 0.5
 UNITS = (
-    ((1, 0), (0, 0), (3, 0)),
-    ((0, 3), (0, 2), (0, 1)),
-    ((1, 3), (1, 1), (2, 1)),
-    ((2, 3), (1, 2), (2, 2)),
-    ((3, 1), (3, 2), (2, 0), (3, 3)),
+    ((0, 3), (0, 1), (3, 0)),
+    ((1, 3), (1, 1), (0, 2)),
+    ((2, 0), (2, 1), (2, 3)),
+    ((0, 0), (1, 2), (2, 2)),
+    ((3, 1), (3, 2), (1, 0), (3, 3)),
 )
 ORDER = (
-    "A0", "P2", "B0", "Q0", "A1", "O0", "F100", "S100", "P3", "A2", "F000", "C0",
-    "B1", "S101", "F110", "S111", "B2", "S110", "A3", "S000", "O1", "O2", "S001", "F010",
-    "C1", "S011", "S010", "R00", "F120", "C2", "S121", "B3", "R01", "S120", "N00", "F130",
-    "S131", "S130", "L00", "F020", "S021", "O3", "N01", "N11", "S020", "N10", "C3", "F030",
-    "S031", "L01", "R11", "S030", "R20", "N20", "R21", "T00", "N21", "F140", "S141", "R10",
-    "S140", "F040", "L20", "S041", "N31", "L21", "R31", "S040", "R30", "N30", "L11", "L10",
-    "L31", "T21", "L30", "T01", "T11", "T20", "T31", "T10", "D31", "D11", "T30", "D10",
-    "D30", "H1", "H0",
+    "A0", "P2", "B0", "Q0", "A1", "O0", "P3", "A2", "F100", "S100", "B1", "S101",
+    "C0", "O1", "B2", "F000", "A3", "S001", "F110", "O2", "S110", "S111", "S000", "N01",
+    "F010", "N00", "C1", "F120", "C2", "S120", "S121", "B3", "S011", "R01", "F130", "S010",
+    "O3", "N10", "N11", "S130", "F020", "R00", "S131", "S021", "S020", "N21", "N20", "C3",
+    "F030", "S030", "R10", "S031", "R21", "R11", "L00", "L01", "F140", "S141", "R20", "S140",
+    "L21", "L10", "F040", "L11", "S041", "R31", "S040", "T01", "R30", "T21", "L20", "N31",
+    "L31", "N30", "L30", "T20", "T11", "D11", "T10", "T31", "D31", "T00", "T30", "D30",
+    "D10", "H1", "H0",
 )
 
 
@@ -57,7 +58,8 @@
     behind = (lax.rem(seg + segments - 1, segments), me)
 
     cols = (pl.ds(0, half), pl.ds(half, half))
-    narrow = width // 4
+    narrow = int(width * NARROW)
+    wide = min(narrow, 768)
     groups = (pl.ds(0, width - narrow), pl.ds(width - narrow, narrow))
     parts = tuple(
         pl.ds(g.start + k * (g.size // 2), g.size // 2) for g in groups for k in range(2)
@@ -217,8 +219,8 @@
     def second(f, unit, h):
         if f == 0:
             arrived(rp.at[band(0, unit), groups[h]], "back", unit, h)
-        for n in range(groups[h].size // narrow):
-            part = pl.ds(groups[h].start + n * narrow, narrow)
+        for n in range(groups[h].size // wide):
+            part = pl.ds(groups[h].start + n * wide, wide)
             value = jnp.dot(act[f, : len(UNITS[unit]) * rows, :], wd[:, part], preferred_element_type=f32)
             if f == 0:
                 value = value + rp[band(0, unit), part].astype(f32)

time: 68 us -> 67.8 us (level)
  no operation moved by 1% of the time
where the time goes in v5:
time: 67.8 us; the launch traced here: 67.7 us
  Pallas kernels  66.9 us (99%)
  local copies, waits for them, and re-layouts  0.72 us (1%)
    pallas_call x1, Pallas kernels, per_device(): pl.pallas_call(body, out_shape=pltpu.VMEM((rows, width), bf16), in_specs=...  66.9 us

profile of v5, /device:TPU:0, one launch (start us, length us, event | category | flops | bytes accessed | tf_op | source)
XLA Modules:
  0.0 67.7 jit_solution(11059145476207942361)
XLA Ops:
  0.0 66.9 %shard_map.64 = bf16[48,3072]{1,0:T(8,128)(2,1)S(1)} custom-call(bf16[48,3072]{1,0:T(8,128)(2,1)} %bitcast.15, bf16[3072,512]{1,0:T(8,128)(2,1)} %bitcast.12, bf16[3072,512]{1,0:T(8,128)(2,1)} %bitcast.13, bf16[512,3072]{1,0:T(8,128)(2,1)} %bitcast.14, s32[6,2,128]{2,1,0:T(2,128)} %bitcast.16, f32[6,2,128]{2,1,0:T(2,128)} %bitcast.17), custom_call_target="tpu_custom_call" | custom-call | tf_op jit(solution)/shard_map/pallas_call | solution.py:335
  67.0 0.7 %copy.8 = bf16[1,2,24,3072]{3,2,1,0:T(8,128)(2,1)} copy(bf16[1,2,24,3072]{3,2,1,0:T(8,128)(2,1)S(1)} %bitcast.11) | data formatting | bytes 589824

commit v6 on v5

--- a/solution.py
+++ b/solution.py
@@ -12,21 +12,21 @@
 SENDERS, RECEIVERS = 13, 63
 NARROW = 0.5
 UNITS = (
-    ((0, 3), (0, 1), (3, 0)),
-    ((1, 3), (1, 1), (0, 2)),
-    ((2, 0), (2, 1), (2, 3)),
-    ((0, 0), (1, 2), (2, 2)),
-    ((3, 1), (3, 2), (1, 0), (3, 3)),
+    ((0, 1), (1, 0), (3, 0)),
+    ((0, 0), (0, 3), (0, 2)),
+    ((1, 1), (2, 1), (1, 3)),
+    ((2, 3), (1, 2), (2, 2)),
+    ((3, 1), (3, 2), (2, 0), (3, 3)),
 )
 ORDER = (
-    "A0", "P2", "B0", "Q0", "A1", "O0", "P3", "A2", "F100", "S100", "B1", "S101",
-    "C0", "O1", "B2", "F000", "A3", "S001", "F110", "O2", "S110", "S111", "S000", "N01",
-    "F010", "N00", "C1", "F120", "C2", "S120", "S121", "B3", "S011", "R01", "F130", "S010",
-    "O3", "N10", "N11", "S130", "F020", "R00", "S131", "S021", "S020", "N21", "N20", "C3",
-    "F030", "S030", "R10", "S031", "R21", "R11", "L00", "L01", "F140", "S141", "R20", "S140",
-    "L21", "L10", "F040", "L11", "S041", "R31", "S040", "T01", "R30", "T21", "L20", "N31",
-    "L31", "N30", "L30", "T20", "T11", "D11", "T10", "T31", "D31", "T00", "T30", "D30",
-    "D10", "H1", "H0",
+    "A0", "P2", "B0", "Q0", "A1", "O0", "P3", "A2", "C0", "F100", "S101", "S100",
+    "B1", "F110", "S110", "S111", "B2", "O1", "A3", "F000", "S001", "S000", "O2", "F010",
+    "S011", "S010", "R01", "C1", "F120", "S120", "C2", "R00", "F020", "B3", "N01", "S121",
+    "F130", "S131", "N00", "S020", "L01", "N10", "S130", "S021", "O3", "N11", "F030", "C3",
+    "S031", "R21", "S030", "R11", "R10", "R20", "N21", "F140", "S141", "T01", "S140", "L00",
+    "L21", "F040", "L11", "N20", "S041", "R31", "S040", "R30", "T21", "N31", "L20", "L31",
+    "N30", "L30", "L10", "T00", "T20", "T11", "T31", "D31", "D11", "T10", "T30", "D10",
+    "D30", "H1", "H0",
 )
 
 

time: 67.8 us -> 67 us (0.988)
  Pallas kernels: 66.9 us -> 66 us
    pallas_call x1, Pallas kernels: 66.9 us -> 66 us  [per_device(): pl.pallas_call(body, out_shape=pltpu.VMEM((rows, width), bf16), in_specs=...]
where the time goes in v6:
time: 67 us; the launch traced here: 66.7 us
  Pallas kernels  66 us (99%)
  local copies, waits for them, and re-layouts  0.72 us (1%)
    pallas_call x1, Pallas kernels, per_device(): pl.pallas_call(body, out_shape=pltpu.VMEM((rows, width), bf16), in_specs=...  66 us

profile of v6, /device:TPU:0, one launch (start us, length us, event | category | flops | bytes accessed | tf_op | source)
XLA Modules:
  0.0 66.7 jit_solution(8832485306894035081)
XLA Ops:
  0.0 66.0 %shard_map.64 = bf16[48,3072]{1,0:T(8,128)(2,1)S(1)} custom-call(bf16[48,3072]{1,0:T(8,128)(2,1)} %bitcast.15, bf16[3072,512]{1,0:T(8,128)(2,1)} %bitcast.12, bf16[3072,512]{1,0:T(8,128)(2,1)} %bitcast.13, bf16[512,3072]{1,0:T(8,128)(2,1)} %bitcast.14, s32[6,2,128]{2,1,0:T(2,128)} %bitcast.16, f32[6,2,128]{2,1,0:T(2,128)} %bitcast.17), custom_call_target="tpu_custom_call" | custom-call | tf_op jit(solution)/shard_map/pallas_call | solution.py:335
  66.0 0.7 %copy.8 = bf16[1,2,24,3072]{3,2,1,0:T(8,128)(2,1)} copy(bf16[1,2,24,3072]{3,2,1,0:T(8,128)(2,1)S(1)} %bitcast.11) | data formatting | bytes 589824
